TPU v7x, 32 devices: a whole 2x2x4 slice. The times are simulated.
32 devices in a mesh: parts: 2 (over y), tm: 4 (over z), space: 4 (over x, core).
Axes of the slice: x: 2, y: 2, z: 4, core: 2. Of those that a mesh axis runs over, the one named last changes fastest.
Arguments:
- rhs: float32 [8, 16, 16, 1024], P(('parts', 'tm'), None, 'space'), parts along dimension 0, may hold values from -24 to 24
- diffusivity: float32 [32, 16, 1024], P('parts', 'space'), parts along dimension 0, may hold values from 0.5 to 2
- velocity: float32 [6], P('parts'), parts along dimension 0, may hold values from -1 to 1
Outputs:
- solution: float32 [8, 16, 16, 1024], P(('parts', 'tm'), None, 'space'), parts along dimension 0
There are 2 independent parts, one for each index of `parts`. A program takes and returns all parts, laid end to end along the dimension named above; each array names one. Nothing has to cross between parts.
All inputs are finite; a program needn't handle non-finite values.
Results may differ from a plain program's by a relative error of at most 0.0002.
Values sent between devices are 32-bit elements; how exact they have to be, the bound alone decides.
No kernel may reach another device: no remote copies, remote signals or barrier semaphores. Data moves between devices by JAX's collectives and lax.ppermute only.
A program may use at most 64 MiB of HBM per device.

v0:
```python
import math
import jax
import jax.numpy as jnp
from jax import lax
from jax.sharding import PartitionSpec as P

circ_alpha = 0.1
relax_weights = (
    1.0 / (1.0 - 0.5 * math.cos(math.pi / 8.0)),
    1.0 / (1.0 - 0.5 * math.cos(3.0 * math.pi / 8.0)),
    1.0 / (1.0 - 0.5 * math.cos(5.0 * math.pi / 8.0)),
    1.0 / (1.0 - 0.5 * math.cos(7.0 * math.pi / 8.0)),
)


def padded(shard, sides, width):
    for axis, dim in sides:
        size, length = (lax.axis_size(axis), shard.shape[dim])
        up = [(i, (i + 1) % size) for i in range(size - 1)]
        down = [(j, i) for i, j in up]
        last = lax.slice_in_dim(shard, length - width, length, axis=dim)
        initial = lax.slice_in_dim(shard, 0, width, axis=dim)
        before = lax.ppermute(last, axis, up)
        after = lax.ppermute(initial, axis, down)
        shard = jnp.concatenate([before, shard, after], axis=dim)
    return shard


def stencil(extended, diffusivity, diag_re, diag_im, velocity):
    center = extended[:, :, :, 1:-1, :]
    upper_y = extended[:, :, :, 2:, :]
    lower_y = extended[:, :, :, :-2, :]
    zero_z = jnp.zeros_like(center[:, :, :1])
    upper_z = jnp.concatenate([center[:, :, 1:], zero_z], axis=2)
    lower_z = jnp.concatenate([zero_z, center[:, :, :-1]], axis=2)
    zero_x = jnp.zeros_like(center[:, :, :, :, :1])
    upper_x = jnp.concatenate([center[:, :, :, :, 1:], zero_x], axis=4)
    lower_x = jnp.concatenate([zero_x, center[:, :, :, :, :-1]], axis=4)
    coefficient = diffusivity[None, None]
    half_velocity = 0.5 * velocity
    beside = (coefficient - half_velocity[0]) * upper_z + (coefficient + half_velocity[0]) * lower_z
    beside = (
        beside
        + (coefficient - half_velocity[1]) * upper_y
        + (coefficient + half_velocity[1]) * lower_y
    )
    beside = (
        beside
        + (coefficient - half_velocity[2]) * upper_x
        + (coefficient + half_velocity[2]) * lower_x
    )
    denominator = diag_re + 6.0 * diffusivity
    center_re = center[:, 0]
    center_im = center[:, 1]
    total_re = denominator * center_re - diag_im * center_im
    total_im = denominator * center_im + diag_im * center_re
    return jnp.stack([total_re, total_im], axis=1) - beside


def divide(residual, diffusivity, diag_re, diag_im):
    denominator = diag_re + 6.0 * diffusivity
    modulus = denominator * denominator + diag_im * diag_im
    residual_re = residual[:, 0]
    residual_im = residual[:, 1]
    quotient_re = (residual_re * denominator + residual_im * diag_im) / modulus
    quotient_im = (residual_im * denominator - residual_re * diag_im) / modulus
    return jnp.stack([quotient_re, quotient_im], axis=1)


def highest(left, right):
    return jnp.dot(left, right, precision=lax.Precision.HIGHEST, preferred_element_type=jnp.float32)


def twiddle(row_index, column_index, length):
    product = row_index[:, None] * column_index[None, :] % length
    phase_table = product.astype(jnp.float32) * (2.0 * math.pi / length)
    return (jnp.cos(phase_table), jnp.sin(phase_table))


def local(rhs, diffusivity, velocity):
    local_steps, depth, rows_y, rows_x = rhs.shape
    length = local_steps * lax.axis_size("tm")
    first_step = lax.axis_index("tm") * local_steps
    own_index = first_step + jnp.arange(local_steps, dtype=jnp.int32)
    log_alpha = math.log(circ_alpha) / length
    cell_count = depth * rows_y * rows_x
    scaled = (
        rhs.reshape(local_steps, cell_count)
        * jnp.exp(own_index.astype(jnp.float32) * log_alpha)[:, None]
    )
    regrouped = lax.all_to_all(scaled, "tm", split_axis=1, concat_axis=0, tiled=True)
    full_index = jnp.arange(length, dtype=jnp.int32)
    cosine_table, sine_table = twiddle(full_index, full_index, length)
    spectrum_re = highest(cosine_table, regrouped)
    spectrum_im = -highest(sine_table, regrouped)
    source_re, source_im = (
        lax.all_to_all(spectrum_re, "tm", split_axis=0, concat_axis=1, tiled=True),
        lax.all_to_all(spectrum_im, "tm", split_axis=0, concat_axis=1, tiled=True),
    )
    source = jnp.stack([source_re, source_im], axis=1).reshape(
        local_steps, 2, depth, rows_y, rows_x
    )
    phase_angle = own_index.astype(jnp.float32) * (2.0 * math.pi / length)
    shift_factor = circ_alpha ** (1.0 / length)
    diag_re = (1.0 - shift_factor * jnp.cos(phase_angle))[:, None, None, None]
    diag_im = (shift_factor * jnp.sin(phase_angle))[:, None, None, None]
    field = relax_weights[0] * divide(source, diffusivity, diag_re, diag_im)
    for weight in relax_weights[1:]:
        extended = padded(field, (("space", 3),), 1)
        applied = stencil(extended, diffusivity, diag_re, diag_im, velocity)
        field = field + weight * divide(source - applied, diffusivity, diag_re, diag_im)
    field_re = field[:, 0].reshape(local_steps, cell_count)
    field_im = field[:, 1].reshape(local_steps, cell_count)
    mixed_re, mixed_im = (
        lax.all_to_all(field_re, "tm", split_axis=1, concat_axis=0, tiled=True),
        lax.all_to_all(field_im, "tm", split_axis=1, concat_axis=0, tiled=True),
    )
    values = (highest(cosine_table, mixed_re) - highest(sine_table, mixed_im)) / length
    restored = lax.all_to_all(values, "tm", split_axis=0, concat_axis=1, tiled=True)
    result = restored * jnp.exp(-own_index.astype(jnp.float32) * log_alpha)[:, None]
    return result.reshape(local_steps, depth, rows_y, rows_x)


def solution(mesh):
    return jax.shard_map(
        local,
        mesh=mesh,
        in_specs=(P(("parts", "tm"), None, "space", None), P("parts", "space", None), P("parts")),
        out_specs=P(("parts", "tm"), None, "space", None),
        check_vma=False,
    )
```

profile of v0, /device:TPU:0, one launch (start us, length us, event | category | flops | bytes accessed | tf_op | source)
XLA Modules:
  0.0 120.9 jit_solution(13436231676874819901)
XLA Ops:
  0.0 1.0 broadcast_multiply_fusion
  1.4 15.0 %all_to_all.84 = f32[1,4,16384]{2,0,1:T(1,128)S(1)} all-to-all(f32[1,4,16384]{2,0,1:T(1,128)S(1)} %mul.497), channel_id=1, replica_groups=mesh['parts'=2,'tm'=4,'space'=4] {'tm'}, dimensions={1} | all-to-all | bytes 524288 | tf_op jit(solution)/shard_map/all_to_all | solution.py:91
  16.4 0.7 convolution_bitcast_fusion
  17.1 1.0 copy.4
  18.1 3.4 %all-to-all-start.1 = ((f32[4,1,16384]{2,1,0:T(1,128)}), f32[4,1,16384]{2,1,0:T(1,128)S(1)}, u32[]{:S(2)}, u32[]{:S(2)}) async-start(f32[4,1,16384]{2,1,0:T(1,128)} %copy.4), calls=%async_computation.1 | async-start | bytes 524288 | tf_op jit(solution)/shard_map/all_to_all | solution.py:97
  21.5 0.7 fusion.2
  22.2 1.0 copy.5
  23.2 6.3 %all-to-all-done.1 = f32[4,1,16384]{2,1,0:T(1,128)S(1)} async-done(((f32[4,1,16384]{2,1,0:T(1,128)}), f32[4,1,16384]{2,1,0:T(1,128)S(1)}, u32[]{:S(2)}, u32[]{:S(2)}) %all-to-all-start.1) | async-done | bytes 262176 | tf_op jit(solution)/shard_map/all_to_all | solution.py:97
  29.5 3.4 %all-to-all-start.2 = ((f32[4,1,16384]{2,1,0:T(1,128)}), f32[4,1,16384]{2,1,0:T(1,128)S(1)}, u32[]{:S(2)}, u32[]{:S(2)}) async-start(f32[4,1,16384]{2,1,0:T(1,128)} %copy.5), calls=%async_computation.2 | async-start | bytes 524288 | tf_op jit(solution)/shard_map/all_to_all | solution.py:98
  33.0 0.6 copy-done.4
  33.7 0.6 fusion.83
  34.3 0.7 reduce
  35.1 0.9 stack.75
  36.2 3.4 %all-to-all-done.2 = f32[4,1,16384]{2,1,0:T(1,128)S(1)} async-done(((f32[4,1,16384]{2,1,0:T(1,128)}), f32[4,1,16384]{2,1,0:T(1,128)S(1)}, u32[]{:S(2)}, u32[]{:S(2)}) %all-to-all-start.2) | async-done | bytes 262176 | tf_op jit(solution)/shard_map/all_to_all | solution.py:98
  39.6 0.7 reduce.1
  41.4 2.3 %fusion.38 = (f32[1,1,16,4,1024]{4,3,2,1,0:T(4,128)S(1)}, f32[1,1,16,4,1024]{4,3,2,1,0:T(4,128)S(1)}, f32[16,4,1024]{2,1,0:T(4,128)S(1)}, f32[16,4,1024]{2,1,0:T...) fusion(f32[16,4,1024]{2,1,0:T(4,128)S(1)} %squeeze.67, ...), kind=kLoop, calls=%fused_computation.79 | loop fusion | flops 1179648 | bytes 2883608 | tf_op jit(solution)/shard_map/stack | solution.py:67
  43.9 0.9 fusion.82
  44.8 1.0 subtract_bitcast_fusion.2
  45.8 1.2 fusion.80
  47.0 1.3 %fusion.81 = (f32[1,2,16,4,1023]{4,3,2,1,0:T(4,128)}, f32[1,2,16,4,1023]{4,3,2,1,0:T(4,128)}) fusion(f32[1,2,16,4,1024]{4,3,2,1,0:T(4,128)S(1)} %maximum_multiply_fusion), kind=kLoop, calls=%fused_computation.131 | loop fusion | bytes 2095104 | tf_op jit(solution)/shard_map/slice | solution.py:37
  48.3 1.3 %collective-permute-start = (f32[1,2,16,1,1024]{4,3,2,1,0:T(1,128)}, f32[1,2,16,1,1024]{4,3,2,1,0:T(1,128)S(1)}, u32[]{:S(2)}, u32[]{:S(2)}) collective-permute-start(f32[1,2,16,1,1024]{4,3,2,1,0:T(1,128)} %get-tuple-element.37), channel_id=1, source_target_pairs={{1,0},{2,1},{3,2},{5,4},{6,5},{7,6},{9,8},{10,9},{11,10},{13,12},{... | collective-permute-start | bytes 393224 | tf_op jit(solution)/shard_map/ppermute | solution.py:24
  49.6 3.7 %collective-permute-start.1 = (f32[1,2,16,1,1024]{4,3,2,1,0:T(1,128)}, f32[1,2,16,1,1024]{4,3,2,1,0:T(1,128)}, u32[]{:S(2)}, u32[]{:S(2)}) collective-permute-start(f32[1,2,16,1,1024]{4,3,2,1,0:T(1,128)} %get-tuple-element.38), channel_id=1, source_target_pairs={{0,1},{1,2},{2,3},{4,5},{5,6},{6,7},{8,9},{9,10},{10,11},{12,13},{... | collective-permute-start | bytes 393224 | tf_op jit(solution)/shard_map/ppermute | solution.py:23
  53.3 1.9 %stack.76 = f32[1,1,16,4,1024]{4,3,2,1,0:T(4,128)} reshape(f32[4,16384]{1,0:T(4,128)} %copy-done.1) | data formatting | bytes 524288 | tf_op jit(solution)/shard_map/stack | solution.py:100
  55.1 1.0 constant_dynamic-update-slice_fusion
  56.3 2.8 %fusion.24 = f32[1,2,16,4,1024]{4,3,2,1,0:T(4,128)S(1)} fusion(f32[1,2,16,4,1024]{4,3,2,1,0:T(4,128)S(1)} %constant_dynamic-update-slice_fusion, f32[1,2,16,4,1024]{4,3,2,1,0:T(4,128)S(1)} %maximum_multiply_fusion, f32[1,2,16,1,1024]{4,3,2,1,0:T(1,128)} %collective-permute-done.1, f32[1,2,16,1,1024]{4,3,2,1,0:T(1,128)S(1)} %collective-permute-done, ...), kind=kLoop, calls=%fused_computation.32 | loop fusion | flops 2097152 | bytes 5962752 | tf_op jit(solution)/shard_map/sub | solution.py:111
  60.5 1.3 %collective-permute-start.2 = (f32[1,2,16,1,1024]{4,3,2,1,0:T(1,128)S(1)}, f32[1,2,16,1,1024]{4,3,2,1,0:T(1,128)S(1)}, u32[]{:S(2)}, u32[]{:S(2)}) collective-permute-start(f32[1,2,16,1,1024]{4,3,2,1,0:T(1,128)S(1)} %get-tuple-element.31), channel_id=1, source_target_pairs={{1,0},{2,1},{3,2},{5,4},{6,5},{7,6},{9,8},{10,9},{11,10},{13,12},{... | collective-permute-start | bytes 393224 | tf_op jit(solution)/shard_map/ppermute | solution.py:24
  61.8 3.2 %collective-permute-start.3 = (f32[1,2,16,1,1024]{4,3,2,1,0:T(1,128)S(1)}, f32[1,2,16,1,1024]{4,3,2,1,0:T(1,128)S(1)}, u32[]{:S(2)}, u32[]{:S(2)}) collective-permute-start(f32[1,2,16,1,1024]{4,3,2,1,0:T(1,128)S(1)} %get-tuple-element.32), channel_id=1, source_target_pairs={{0,1},{1,2},{2,3},{4,5},{5,6},{6,7},{8,9},{9,10},{10,11},{12,13},{... | collective-permute-start | bytes 393224 | tf_op jit(solution)/shard_map/ppermute | solution.py:23
  65.2 0.6 collective-permute-done.3
  65.8 1.2 %fusion.16 = f32[1,2,16,4,1024]{4,3,2,1,0:T(4,128)S(1)} fusion(f32[1,2,16,4,1024]{4,3,2,1,0:T(4,128)S(1)} %constant_dynamic-update-slice_fusion, f32[1,2,16,4,1024]{4,3,2,1,0:T(4,128)S(1)} %fusion.27, f32[1,2,16,1,1024]{4,3,2,1,0:T(1,128)S(1)} %collective-permute-done.3, f32[1,2,16,1,1024]{4,3,2,1,0:T(1,128)S(1)} %collective-permute-done.2, ...), kind=kLoop, calls=%fused_computation.22 | loop fusion | flops 2097152 | bytes 5962752 | tf_op jit(solution)/shard_map/sub | solution.py:111
  67.3 0.5 fusion.28
  68.6 1.3 %collective-permute-start.4 = (f32[1,2,16,1,1024]{4,3,2,1,0:T(1,128)S(1)}, f32[1,2,16,1,1024]{4,3,2,1,0:T(1,128)S(1)}, u32[]{:S(2)}, u32[]{:S(2)}) collective-permute-start(f32[1,2,16,1,1024]{4,3,2,1,0:T(1,128)S(1)} %get-tuple-element.25), channel_id=1, source_target_pairs={{1,0},{2,1},{3,2},{5,4},{6,5},{7,6},{9,8},{10,9},{11,10},{13,12},{... | collective-permute-start | bytes 393224 | tf_op jit(solution)/shard_map/ppermute | solution.py:24
  69.9 5.2 %collective-permute-start.5 = (f32[1,2,16,1,1024]{4,3,2,1,0:T(1,128)S(1)}, f32[1,2,16,1,1024]{4,3,2,1,0:T(1,128)S(1)}, u32[]{:S(2)}, u32[]{:S(2)}) collective-permute-start(f32[1,2,16,1,1024]{4,3,2,1,0:T(1,128)S(1)} %get-tuple-element.26), channel_id=1, source_target_pairs={{0,1},{1,2},{2,3},{4,5},{5,6},{6,7},{8,9},{9,10},{10,11},{12,13},{... | collective-permute-start | bytes 393224 | tf_op jit(solution)/shard_map/ppermute | solution.py:23
  75.3 0.8 collective-permute-done.5
  76.1 1.2 %fusion.8 = f32[1,2,16,4,1024]{4,3,2,1,0:T(4,128)S(1)} fusion(f32[1,2,16,4,1024]{4,3,2,1,0:T(4,128)S(1)} %constant_dynamic-update-slice_fusion, f32[1,2,16,4,1024]{4,3,2,1,0:T(4,128)S(1)} %fusion.28, f32[1,2,16,1,1024]{4,3,2,1,0:T(1,128)S(1)} %collective-permute-done.5, f32[1,2,16,1,1024]{4,3,2,1,0:T(1,128)S(1)} %collective-permute-done.4, ...), kind=kLoop, calls=%fused_computation.12 | loop fusion | flops 2097152 | bytes 5962752 | tf_op jit(solution)/shard_map/sub | solution.py:111
  77.6 0.6 fusion.29
  78.2 1.1 all_to_all.70
  79.3 3.4 %all-to-all-start.3 = ((f32[1,4,16384]{2,0,1:T(1,128)}), f32[1,4,16384]{2,0,1:T(1,128)S(1)}, u32[]{:S(2)}, u32[]{:S(2)}) async-start(f32[1,4,16384]{2,0,1:T(1,128)} %all_to_all.70), calls=%async_computation.3 | async-start | bytes 524288 | tf_op jit(solution)/shard_map/all_to_all | solution.py:115
  82.7 1.1 all_to_all.73
  83.8 5.8 %all-to-all-done.3 = f32[1,4,16384]{2,0,1:T(1,128)S(1)} async-done(((f32[1,4,16384]{2,0,1:T(1,128)}), f32[1,4,16384]{2,0,1:T(1,128)S(1)}, u32[]{:S(2)}, u32[]{:S(2)}) %all-to-all-start.3) | async-done | bytes 262176 | tf_op jit(solution)/shard_map/all_to_all | solution.py:115
  89.5 5.2 %all-to-all-start.4 = ((f32[1,4,16384]{2,0,1:T(1,128)}), f32[1,4,16384]{2,0,1:T(1,128)S(1)}, u32[]{:S(2)}, u32[]{:S(2)}) async-start(f32[1,4,16384]{2,0,1:T(1,128)} %all_to_all.73), calls=%async_computation.4 | async-start | bytes 524288 | tf_op jit(solution)/shard_map/all_to_all | solution.py:116
  94.7 0.7 fusion.32
  95.4 8.0 %all-to-all-done.4 = f32[1,4,16384]{2,0,1:T(1,128)S(1)} async-done(((f32[1,4,16384]{2,0,1:T(1,128)}), f32[1,4,16384]{2,0,1:T(1,128)S(1)}, u32[]{:S(2)}, u32[]{:S(2)}) %all-to-all-start.4) | async-done | bytes 262176 | tf_op jit(solution)/shard_map/all_to_all | solution.py:116
  103.4 0.7 fusion.1
  104.1 1.0 copy.6
  105.1 4.0 %all-to-all-start.5 = ((f32[4,1,16384]{2,1,0:T(1,128)}), f32[4,1,16384]{2,1,0:T(1,128)S(1)}, u32[]{:S(2)}, u32[]{:S(2)}) async-start(f32[4,1,16384]{2,1,0:T(1,128)} %copy.6), calls=%async_computation.5 | async-start | bytes 524288 | tf_op jit(solution)/shard_map/all_to_all | solution.py:119
  109.2 10.0 %all-to-all-done.5 = f32[4,1,16384]{2,1,0:T(1,128)S(1)} async-done(((f32[4,1,16384]{2,1,0:T(1,128)}), f32[4,1,16384]{2,1,0:T(1,128)S(1)}, u32[]{:S(2)}, u32[]{:S(2)}) %all-to-all-start.5) | async-done | bytes 262176 | tf_op jit(solution)/shard_map/all_to_all | solution.py:119
  119.2 0.7 multiply_reduce_fusion
  120.0 0.9 mul.572
  (32 shorter events, 4.9 us)
Async XLA Ops:
  18.1 11.4 %all-to-all-start.1 = ((f32[4,1,16384]{2,1,0:T(1,128)}), f32[4,1,16384]{2,1,0:T(1,128)S(1)}, u32[]{:S(2)}, u32[]{:S(2)}) async-start(f32[4,1,16384]{2,1,0:T(1,128)} %copy.4), calls=%async_computation.1 | async-start | bytes 524288 | tf_op jit(solution)/shard_map/all_to_all | solution.py:97
  29.5 10.2 %all-to-all-start.2 = ((f32[4,1,16384]{2,1,0:T(1,128)}), f32[4,1,16384]{2,1,0:T(1,128)S(1)}, u32[]{:S(2)}, u32[]{:S(2)}) async-start(f32[4,1,16384]{2,1,0:T(1,128)} %copy.5), calls=%async_computation.2 | async-start | bytes 524288 | tf_op jit(solution)/shard_map/all_to_all | solution.py:98
  33.0 0.7 copy-start.4
  40.3 0.7 copy-start.1
  40.3 1.0 copy-start
  47.0 6.3 %copy-start.3 = (f32[1,1,16,4,1024]{4,3,2,1,0:T(4,128)S(1)}, f32[1,1,16,4,1024]{4,3,2,1,0:T(4,128)}, u32[]{:S(2)}) copy-start(f32[1,1,16,4,1024]{4,3,2,1,0:T(4,128)} %stack.75) | copy-start | bytes 786436
  48.3 7.9 %collective-permute-start = (f32[1,2,16,1,1024]{4,3,2,1,0:T(1,128)}, f32[1,2,16,1,1024]{4,3,2,1,0:T(1,128)S(1)}, u32[]{:S(2)}, u32[]{:S(2)}) collective-permute-start(f32[1,2,16,1,1024]{4,3,2,1,0:T(1,128)} %get-tuple-element.37), channel_id=1, source_target_pairs={{1,0},{2,1},{3,2},{5,4},{6,5},{7,6},{9,8},{10,9},{11,10},{13,12},{... | collective-permute-start | bytes 393224 | tf_op jit(solution)/shard_map/ppermute | solution.py:24
  49.6 6.7 %collective-permute-start.1 = (f32[1,2,16,1,1024]{4,3,2,1,0:T(1,128)}, f32[1,2,16,1,1024]{4,3,2,1,0:T(1,128)}, u32[]{:S(2)}, u32[]{:S(2)}) collective-permute-start(f32[1,2,16,1,1024]{4,3,2,1,0:T(1,128)} %get-tuple-element.38), channel_id=1, source_target_pairs={{0,1},{1,2},{2,3},{4,5},{5,6},{6,7},{8,9},{9,10},{10,11},{12,13},{... | collective-permute-start | bytes 393224 | tf_op jit(solution)/shard_map/ppermute | solution.py:23
  55.1 1.1 copy-start.2
  60.5 4.7 %collective-permute-start.2 = (f32[1,2,16,1,1024]{4,3,2,1,0:T(1,128)S(1)}, f32[1,2,16,1,1024]{4,3,2,1,0:T(1,128)S(1)}, u32[]{:S(2)}, u32[]{:S(2)}) collective-permute-start(f32[1,2,16,1,1024]{4,3,2,1,0:T(1,128)S(1)} %get-tuple-element.31), channel_id=1, source_target_pairs={{1,0},{2,1},{3,2},{5,4},{6,5},{7,6},{9,8},{10,9},{11,10},{13,12},{... | collective-permute-start | bytes 393224 | tf_op jit(solution)/shard_map/ppermute | solution.py:24
  61.8 4.0 %collective-permute-start.3 = (f32[1,2,16,1,1024]{4,3,2,1,0:T(1,128)S(1)}, f32[1,2,16,1,1024]{4,3,2,1,0:T(1,128)S(1)}, u32[]{:S(2)}, u32[]{:S(2)}) collective-permute-start(f32[1,2,16,1,1024]{4,3,2,1,0:T(1,128)S(1)} %get-tuple-element.32), channel_id=1, source_target_pairs={{0,1},{1,2},{2,3},{4,5},{5,6},{6,7},{8,9},{9,10},{10,11},{12,13},{... | collective-permute-start | bytes 393224 | tf_op jit(solution)/shard_map/ppermute | solution.py:23
  68.6 6.7 %collective-permute-start.4 = (f32[1,2,16,1,1024]{4,3,2,1,0:T(1,128)S(1)}, f32[1,2,16,1,1024]{4,3,2,1,0:T(1,128)S(1)}, u32[]{:S(2)}, u32[]{:S(2)}) collective-permute-start(f32[1,2,16,1,1024]{4,3,2,1,0:T(1,128)S(1)} %get-tuple-element.25), channel_id=1, source_target_pairs={{1,0},{2,1},{3,2},{5,4},{6,5},{7,6},{9,8},{10,9},{11,10},{13,12},{... | collective-permute-start | bytes 393224 | tf_op jit(solution)/shard_map/ppermute | solution.py:24
  69.9 6.2 %collective-permute-start.5 = (f32[1,2,16,1,1024]{4,3,2,1,0:T(1,128)S(1)}, f32[1,2,16,1,1024]{4,3,2,1,0:T(1,128)S(1)}, u32[]{:S(2)}, u32[]{:S(2)}) collective-permute-start(f32[1,2,16,1,1024]{4,3,2,1,0:T(1,128)S(1)} %get-tuple-element.26), channel_id=1, source_target_pairs={{0,1},{1,2},{2,3},{4,5},{5,6},{6,7},{8,9},{9,10},{10,11},{12,13},{... | collective-permute-start | bytes 393224 | tf_op jit(solution)/shard_map/ppermute | solution.py:23
  79.3 10.3 %all-to-all-start.3 = ((f32[1,4,16384]{2,0,1:T(1,128)}), f32[1,4,16384]{2,0,1:T(1,128)S(1)}, u32[]{:S(2)}, u32[]{:S(2)}) async-start(f32[1,4,16384]{2,0,1:T(1,128)} %all_to_all.70), calls=%async_computation.3 | async-start | bytes 524288 | tf_op jit(solution)/shard_map/all_to_all | solution.py:115
  89.5 13.9 %all-to-all-start.4 = ((f32[1,4,16384]{2,0,1:T(1,128)}), f32[1,4,16384]{2,0,1:T(1,128)S(1)}, u32[]{:S(2)}, u32[]{:S(2)}) async-start(f32[1,4,16384]{2,0,1:T(1,128)} %all_to_all.73), calls=%async_computation.4 | async-start | bytes 524288 | tf_op jit(solution)/shard_map/all_to_all | solution.py:116
  105.1 14.1 %all-to-all-start.5 = ((f32[4,1,16384]{2,1,0:T(1,128)}), f32[4,1,16384]{2,1,0:T(1,128)S(1)}, u32[]{:S(2)}, u32[]{:S(2)}) async-start(f32[4,1,16384]{2,1,0:T(1,128)} %copy.6), calls=%async_computation.5 | async-start | bytes 524288 | tf_op jit(solution)/shard_map/all_to_all | solution.py:119
where the time goes:
time: 122 us; the launch traced here: 121 us
  starting transfers between devices  35.5 us (29%)
  waiting for transfers between devices  34.8 us (29%)
  local copies, waits for them, and re-layouts  17.9 us (15%)
  blocking collectives  15 us (12%)
  other arithmetic  14.3 us (12%)
  matrix products  2.78 us (2%)
    all_to_all x1, blocking collectives, local(): lax.all_to_all(scaled, 'tm', split_axis=1, concat_axis=0, tiled=True)  15 us
    ppermute x3, starting transfers between devices, padded(): before = lax.ppermute(last, axis, up)  12.1 us
    all_to_all x1, waiting for transfers between devices, local(): lax.all_to_all(values, 'tm', split_axis=0, concat_axis=1, tiled=True)  10 us
    all_to_all x1, waiting for transfers between devices, local(): lax.all_to_all(field_im, 'tm', split_axis=1, concat_axis=0, tiled=True)  8 us
    all_to_all x1, waiting for transfers between devices, local(): lax.all_to_all(spectrum_re, 'tm', split_axis=0, concat_axis=1, tiled=True)  6.28 us
    all_to_all x1, waiting for transfers between devices, local(): lax.all_to_all(field_re, 'tm', split_axis=1, concat_axis=0, tiled=True)  5.78 us
    sub x3, other arithmetic, local(): source - applied  5.27 us
    all_to_all x1, starting transfers between devices, local(): lax.all_to_all(field_im, 'tm', split_axis=1, concat_axis=0, tiled=True)  5.19 us
  transfers between devices with their start and end apart: 11, of which 7 were waited for; matrix products, arithmetic and copies ran while one was open for 7% of the time, Pallas kernels for 0%

commit v1 on v0

--- a/solution.py
+++ b/solution.py
@@ -11,6 +11,29 @@
     1.0 / (1.0 - 0.5 * math.cos(5.0 * math.pi / 8.0)),
     1.0 / (1.0 - 0.5 * math.cos(7.0 * math.pi / 8.0)),
 )
+
+
+def in_blocks(x, dim, peers):
+    dims = x.shape
+    parts = x.reshape(*dims[:dim], peers, dims[dim] // peers, *dims[dim + 1 :])
+    return jnp.moveaxis(parts, dim, 0)
+
+
+def joined_along(tiles, dim):
+    tiles = jnp.moveaxis(tiles, 0, dim)
+    shape = tiles.shape
+    return tiles.reshape(*shape[:dim], shape[dim] * shape[dim + 1], *shape[dim + 2 :])
+
+
+def pairwise_exchange(x, axis, split_dim, concat_dim):
+    size, here = (lax.axis_size(axis), lax.axis_index(axis))
+    parts = in_blocks(x, split_dim, size)
+    gathered = [parts[here]]
+    for lap in range(1, size):
+        sent = parts[here ^ lap]
+        gathered.append(lax.ppermute(sent, axis, [(i, i ^ lap) for i in range(size)]))
+    parts = jnp.stack(gathered)[here ^ jnp.arange(size)]
+    return joined_along(parts, concat_dim)
 
 
 def padded(shard, sides, width):
@@ -95,7 +118,7 @@
     spectrum_im = -highest(sine_table, regrouped)
     source_re, source_im = (
         lax.all_to_all(spectrum_re, "tm", split_axis=0, concat_axis=1, tiled=True),
-        lax.all_to_all(spectrum_im, "tm", split_axis=0, concat_axis=1, tiled=True),
+        pairwise_exchange(spectrum_im, "tm", 0, 1),
     )
     source = jnp.stack([source_re, source_im], axis=1).reshape(
         local_steps, 2, depth, rows_y, rows_x

time: 122 us -> 112 us (0.918)
  blocking collectives: 15 us -> 0 us
  starting transfers between devices: 35.5 us -> 44.5 us
  local copies, waits for them, and re-layouts: 17.9 us -> 12.4 us
  waiting for transfers between devices: 34.8 us -> 38.8 us
  other arithmetic: 14.3 us -> 11.6 us
    all_to_all x1 -> x0, blocking collectives: 15 us -> none  [local(): lax.all_to_all(scaled, 'tm', split_axis=1, concat_axis=0, tiled=True)]
    ppermute x0 -> x3, starting transfers between devices: none -> 4.45 us  [pairwise_exchange(): lax.ppermute(sent, axis, [(i, i ^ lap) for i in range(size)])]
    all_to_all x1, waiting for transfers between devices: 3.39 us -> 7.38 us  [local(): lax.all_to_all(scaled, 'tm', split_axis=1, concat_axis=0, tiled=True)]
    another operation x3, local copies, waits for them, and re-layouts: 3.85 us -> 0.49 us  [local(): jnp.stack([source_re, source_im], axis=1)]
    all_to_all x1, starting transfers between devices: 3.4 us -> 6.35 us  [local(): lax.all_to_all(scaled, 'tm', split_axis=1, concat_axis=0, tiled=True)]
    ppermute x3, starting transfers between devices: 12.1 us -> 13.8 us  [padded(): before = lax.ppermute(last, axis, up)]
    sub x3, other arithmetic: 5.27 us -> 3.68 us  [local(): source - applied]
  transfers between devices with their start and end apart: 11 -> 14, of which waited for: 7 -> 8; matrix products, arithmetic and copies ran while one was open for 7% -> 4% of each run, Pallas kernels for 0% -> 0%
where the time goes in v1:
time: 112 us; the launch traced here: 111 us
  starting transfers between devices  44.5 us (40%)
  waiting for transfers between devices  38.8 us (35%)
  local copies, waits for them, and re-layouts  12.4 us (11%)
  other arithmetic  11.6 us (10%)
  matrix products  2.78 us (2%)
    ppermute x3, starting transfers between devices, padded(): before = lax.ppermute(last, axis, up)  13.8 us
    all_to_all x1, waiting for transfers between devices, local(): lax.all_to_all(values, 'tm', split_axis=0, concat_axis=1, tiled=True)  10 us
    all_to_all x1, waiting for transfers between devices, local(): lax.all_to_all(field_im, 'tm', split_axis=1, concat_axis=0, tiled=True)  8 us
    all_to_all x1, waiting for transfers between devices, local(): lax.all_to_all(scaled, 'tm', split_axis=1, concat_axis=0, tiled=True)  7.38 us
    all_to_all x1, starting transfers between devices, local(): lax.all_to_all(scaled, 'tm', split_axis=1, concat_axis=0, tiled=True)  6.35 us
    all_to_all x1, waiting for transfers between devices, local(): lax.all_to_all(field_re, 'tm', split_axis=1, concat_axis=0, tiled=True)  5.8 us
    all_to_all x1, waiting for transfers between devices, local(): lax.all_to_all(spectrum_re, 'tm', split_axis=0, concat_axis=1, tiled=True)  5.31 us
    all_to_all x1, starting transfers between devices, local(): lax.all_to_all(field_im, 'tm', split_axis=1, concat_axis=0, tiled=True)  5.19 us
  transfers between devices with their start and end apart: 14, of which 8 were waited for; matrix products, arithmetic and copies ran while one was open for 4% of the time, Pallas kernels for 0%

profile of v1, /device:TPU:0, one launch (start us, length us, event | category | flops | bytes accessed | tf_op | source)
XLA Modules:
  0.0 110.8 jit_solution(17991014469948569229)
XLA Ops:
  0.0 1.0 broadcast_multiply_fusion
  1.0 1.1 mul.497
  2.1 6.3 %all-to-all-start = ((f32[1,4,16384]{2,0,1:T(1,128)}), f32[1,4,16384]{2,0,1:T(1,128)S(1)}, u32[]{:S(2)}, u32[]{:S(2)}) async-start(f32[1,4,16384]{2,0,1:T(1,128)} %mul.497), calls=%async_computation | async-start | bytes 524288 | tf_op jit(solution)/shard_map/all_to_all | solution.py:114
  8.7 0.6 copy-done.1
  9.3 0.7 fusion.83
  10.0 7.4 %all-to-all-done = f32[1,4,16384]{2,0,1:T(1,128)S(1)} async-done(((f32[1,4,16384]{2,0,1:T(1,128)}), f32[1,4,16384]{2,0,1:T(1,128)S(1)}, u32[]{:S(2)}, u32[]{:S(2)}) %all-to-all-start) | async-done | bytes 262176 | tf_op jit(solution)/shard_map/all_to_all | solution.py:114
  17.3 0.7 convolution_negate_fusion
  18.3 1.5 %collective-permute-start.2 = (f32[1,16384]{1,0:T(1,128)S(1)}, f32[1,16384]{1,0:T(1,128)S(1)}, u32[]{:S(2)}, u32[]{:S(2)}) collective-permute-start(f32[1,16384]{1,0:T(1,128)S(1)} %get-tuple-element.46), channel_id=1, source_target_pairs={{0,12},{4,8},{8,4},{12,0},{1,13},{5,9},{9,5},{13,1},{2,14},{6,10},... | collective-permute-start | bytes 196616 | tf_op jit(solution)/shard_map/ppermute | solution.py:34
  20.0 2.8 %collective-permute-start = (f32[1,16384]{1,0:T(1,128)S(1)}, f32[1,16384]{1,0:T(1,128)S(1)}, u32[]{:S(2)}, u32[]{:S(2)}) collective-permute-start(f32[1,16384]{1,0:T(1,128)S(1)} %get-tuple-element.48), channel_id=1, source_target_pairs={{0,4},{4,0},{8,12},{12,8},{1,5},{5,1},{9,13},{13,9},{2,6},{6,2},{1... | collective-permute-start | bytes 196616 | tf_op jit(solution)/shard_map/ppermute | solution.py:34
  22.7 0.7 convolution_bitcast_fusion
  23.4 1.0 copy.4
  24.4 3.4 %all-to-all-start.1 = ((f32[4,1,16384]{2,1,0:T(1,128)}), f32[4,1,16384]{2,1,0:T(1,128)S(1)}, u32[]{:S(2)}, u32[]{:S(2)}) async-start(f32[4,1,16384]{2,1,0:T(1,128)} %copy.4), calls=%async_computation.1 | async-start | bytes 524288 | tf_op jit(solution)/shard_map/all_to_all | solution.py:120
  28.1 0.7 gather_fusion
  29.3 5.3 %all-to-all-done.1 = f32[4,1,16384]{2,1,0:T(1,128)S(1)} async-done(((f32[4,1,16384]{2,1,0:T(1,128)}), f32[4,1,16384]{2,1,0:T(1,128)S(1)}, u32[]{:S(2)}, u32[]{:S(2)}) %all-to-all-start.1) | async-done | bytes 262176 | tf_op jit(solution)/shard_map/all_to_all | solution.py:120
  34.6 0.7 reduce
  35.8 0.7 copy-done
  36.5 2.4 %fusion.37 = (f32[1,1,16,4,1024]{4,3,2,1,0:T(4,128)S(1)}, f32[1,1,16,4,1024]{4,3,2,1,0:T(4,128)S(1)}, f32[16,4,1024]{2,1,0:T(4,128)S(1)}, f32[16,4,1024]{2,1,0:T...) fusion(f32[16,4,1024]{2,1,0:T(4,128)S(1)} %squeeze.79, ...), kind=kLoop, calls=%fused_computation.80 | loop fusion | flops 1179648 | bytes 2883608 | tf_op jit(solution)/shard_map/stack | solution.py:90
  39.8 0.4 fusion.81
  40.1 1.3 %collective-permute-start.3 = (f32[1,2,16,1,1024]{4,3,2,1,0:T(1,128)S(1)}, f32[1,2,16,1,1024]{4,3,2,1,0:T(1,128)S(1)}, u32[]{:S(2)}, u32[]{:S(2)}) collective-permute-start(f32[1,2,16,1,1024]{4,3,2,1,0:T(1,128)S(1)} %get-tuple-element.37), channel_id=1, source_target_pairs={{1,0},{2,1},{3,2},{5,4},{6,5},{7,6},{9,8},{10,9},{11,10},{13,12},{... | collective-permute-start | bytes 393224 | tf_op jit(solution)/shard_map/ppermute | solution.py:47
  41.4 3.0 %collective-permute-start.4 = (f32[1,2,16,1,1024]{4,3,2,1,0:T(1,128)S(1)}, f32[1,2,16,1,1024]{4,3,2,1,0:T(1,128)S(1)}, u32[]{:S(2)}, u32[]{:S(2)}) collective-permute-start(f32[1,2,16,1,1024]{4,3,2,1,0:T(1,128)S(1)} %get-tuple-element.38), channel_id=1, source_target_pairs={{0,1},{1,2},{2,3},{4,5},{5,6},{6,7},{8,9},{9,10},{10,11},{12,13},{... | collective-permute-start | bytes 393224 | tf_op jit(solution)/shard_map/ppermute | solution.py:46
  44.5 0.9 collective-permute-done.4
  45.4 1.2 %fusion.23 = f32[1,2,16,4,1024]{4,3,2,1,0:T(4,128)S(1)} fusion(f32[1,2,16,4,1024]{4,3,2,1,0:T(4,128)S(1)} %constant_dynamic-update-slice_fusion, f32[1,2,16,4,1024]{4,3,2,1,0:T(4,128)S(1)} %maximum_multiply_fusion, f32[1,2,16,1,1024]{4,3,2,1,0:T(1,128)S(1)} %collective-permute-done.4, f32[1,2,16,1,1024]{4,3,2,1,0:T(1,128)S(1)} %collective-permute-done.3, ...), kind=kLoop, calls=%fused_computation.32 | loop fusion | flops 2097152 | bytes 5962752 | tf_op jit(solution)/shard_map/sub | solution.py:134
  46.9 0.3 fusion.26
  47.7 0.4 fusion.78
  48.1 1.3 %collective-permute-start.5 = (f32[1,2,16,1,1024]{4,3,2,1,0:T(1,128)S(1)}, f32[1,2,16,1,1024]{4,3,2,1,0:T(1,128)S(1)}, u32[]{:S(2)}, u32[]{:S(2)}) collective-permute-start(f32[1,2,16,1,1024]{4,3,2,1,0:T(1,128)S(1)} %get-tuple-element.31), channel_id=1, source_target_pairs={{1,0},{2,1},{3,2},{5,4},{6,5},{7,6},{9,8},{10,9},{11,10},{13,12},{... | collective-permute-start | bytes 393224 | tf_op jit(solution)/shard_map/ppermute | solution.py:47
  49.4 4.8 %collective-permute-start.6 = (f32[1,2,16,1,1024]{4,3,2,1,0:T(1,128)S(1)}, f32[1,2,16,1,1024]{4,3,2,1,0:T(1,128)S(1)}, u32[]{:S(2)}, u32[]{:S(2)}) collective-permute-start(f32[1,2,16,1,1024]{4,3,2,1,0:T(1,128)S(1)} %get-tuple-element.32), channel_id=1, source_target_pairs={{0,1},{1,2},{2,3},{4,5},{5,6},{6,7},{8,9},{9,10},{10,11},{12,13},{... | collective-permute-start | bytes 393224 | tf_op jit(solution)/shard_map/ppermute | solution.py:46
  54.4 0.6 collective-permute-done.6
  55.0 1.2 %fusion.15 = f32[1,2,16,4,1024]{4,3,2,1,0:T(4,128)S(1)} fusion(f32[1,2,16,4,1024]{4,3,2,1,0:T(4,128)S(1)} %constant_dynamic-update-slice_fusion, f32[1,2,16,4,1024]{4,3,2,1,0:T(4,128)S(1)} %fusion.26, f32[1,2,16,1,1024]{4,3,2,1,0:T(1,128)S(1)} %collective-permute-done.6, f32[1,2,16,1,1024]{4,3,2,1,0:T(1,128)S(1)} %collective-permute-done.5, ...), kind=kLoop, calls=%fused_computation.22 | loop fusion | flops 2097152 | bytes 5962752 | tf_op jit(solution)/shard_map/sub | solution.py:134
  56.4 0.5 fusion.27
  57.4 0.4 fusion.75
  57.7 1.3 %collective-permute-start.7 = (f32[1,2,16,1,1024]{4,3,2,1,0:T(1,128)S(1)}, f32[1,2,16,1,1024]{4,3,2,1,0:T(1,128)S(1)}, u32[]{:S(2)}, u32[]{:S(2)}) collective-permute-start(f32[1,2,16,1,1024]{4,3,2,1,0:T(1,128)S(1)} %get-tuple-element.25), channel_id=1, source_target_pairs={{1,0},{2,1},{3,2},{5,4},{6,5},{7,6},{9,8},{10,9},{11,10},{13,12},{... | collective-permute-start | bytes 393224 | tf_op jit(solution)/shard_map/ppermute | solution.py:47
  59.0 5.9 %collective-permute-start.8 = (f32[1,2,16,1,1024]{4,3,2,1,0:T(1,128)S(1)}, f32[1,2,16,1,1024]{4,3,2,1,0:T(1,128)S(1)}, u32[]{:S(2)}, u32[]{:S(2)}) collective-permute-start(f32[1,2,16,1,1024]{4,3,2,1,0:T(1,128)S(1)} %get-tuple-element.26), channel_id=1, source_target_pairs={{0,1},{1,2},{2,3},{4,5},{5,6},{6,7},{8,9},{9,10},{10,11},{12,13},{... | collective-permute-start | bytes 393224 | tf_op jit(solution)/shard_map/ppermute | solution.py:46
  65.2 0.8 collective-permute-done.8
  66.0 1.2 %fusion.7 = f32[1,2,16,4,1024]{4,3,2,1,0:T(4,128)S(1)} fusion(f32[1,2,16,4,1024]{4,3,2,1,0:T(4,128)S(1)} %constant_dynamic-update-slice_fusion, f32[1,2,16,4,1024]{4,3,2,1,0:T(4,128)S(1)} %fusion.27, f32[1,2,16,1,1024]{4,3,2,1,0:T(1,128)S(1)} %collective-permute-done.8, f32[1,2,16,1,1024]{4,3,2,1,0:T(1,128)S(1)} %collective-permute-done.7, ...), kind=kLoop, calls=%fused_computation.12 | loop fusion | flops 2097152 | bytes 5962752 | tf_op jit(solution)/shard_map/sub | solution.py:134
  67.4 0.6 fusion.28
  68.1 1.1 all_to_all.58
  69.1 3.4 %all-to-all-start.2 = ((f32[1,4,16384]{2,0,1:T(1,128)}), f32[1,4,16384]{2,0,1:T(1,128)S(1)}, u32[]{:S(2)}, u32[]{:S(2)}) async-start(f32[1,4,16384]{2,0,1:T(1,128)} %all_to_all.58), calls=%async_computation.2 | async-start | bytes 524288 | tf_op jit(solution)/shard_map/all_to_all | solution.py:138
  72.6 1.0 all_to_all.61
  73.6 5.8 %all-to-all-done.2 = f32[1,4,16384]{2,0,1:T(1,128)S(1)} async-done(((f32[1,4,16384]{2,0,1:T(1,128)}), f32[1,4,16384]{2,0,1:T(1,128)S(1)}, u32[]{:S(2)}, u32[]{:S(2)}) %all-to-all-start.2) | async-done | bytes 262176 | tf_op jit(solution)/shard_map/all_to_all | solution.py:138
  79.4 5.2 %all-to-all-start.3 = ((f32[1,4,16384]{2,0,1:T(1,128)}), f32[1,4,16384]{2,0,1:T(1,128)S(1)}, u32[]{:S(2)}, u32[]{:S(2)}) async-start(f32[1,4,16384]{2,0,1:T(1,128)} %all_to_all.61), calls=%async_computation.3 | async-start | bytes 524288 | tf_op jit(solution)/shard_map/all_to_all | solution.py:139
  84.6 0.7 fusion.31
  85.3 8.0 %all-to-all-done.3 = f32[1,4,16384]{2,0,1:T(1,128)S(1)} async-done(((f32[1,4,16384]{2,0,1:T(1,128)}), f32[1,4,16384]{2,0,1:T(1,128)S(1)}, u32[]{:S(2)}, u32[]{:S(2)}) %all-to-all-start.3) | async-done | bytes 262176 | tf_op jit(solution)/shard_map/all_to_all | solution.py:139
  93.3 0.7 fusion.1
  94.0 1.0 copy.5
  95.0 4.0 %all-to-all-start.4 = ((f32[4,1,16384]{2,1,0:T(1,128)}), f32[4,1,16384]{2,1,0:T(1,128)S(1)}, u32[]{:S(2)}, u32[]{:S(2)}) async-start(f32[4,1,16384]{2,1,0:T(1,128)} %copy.5), calls=%async_computation.4 | async-start | bytes 524288 | tf_op jit(solution)/shard_map/all_to_all | solution.py:142
  99.1 10.0 %all-to-all-done.4 = f32[4,1,16384]{2,1,0:T(1,128)S(1)} async-done(((f32[4,1,16384]{2,1,0:T(1,128)}), f32[4,1,16384]{2,1,0:T(1,128)S(1)}, u32[]{:S(2)}, u32[]{:S(2)}) %all-to-all-start.4) | async-done | bytes 262176 | tf_op jit(solution)/shard_map/all_to_all | solution.py:142
  109.1 0.7 multiply_reduce_fusion
  109.8 0.9 mul.572
  (34 shorter events, 4.5 us)
Async XLA Ops:
  2.1 15.3 %all-to-all-start = ((f32[1,4,16384]{2,0,1:T(1,128)}), f32[1,4,16384]{2,0,1:T(1,128)S(1)}, u32[]{:S(2)}, u32[]{:S(2)}) async-start(f32[1,4,16384]{2,0,1:T(1,128)} %mul.497), calls=%async_computation | async-start | bytes 524288 | tf_op jit(solution)/shard_map/all_to_all | solution.py:114
  8.6 0.7 copy-start.1
  18.3 9.5 %collective-permute-start.2 = (f32[1,16384]{1,0:T(1,128)S(1)}, f32[1,16384]{1,0:T(1,128)S(1)}, u32[]{:S(2)}, u32[]{:S(2)}) collective-permute-start(f32[1,16384]{1,0:T(1,128)S(1)} %get-tuple-element.46), channel_id=1, source_target_pairs={{0,12},{4,8},{8,4},{12,0},{1,13},{5,9},{9,5},{13,1},{2,14},{6,10},... | collective-permute-start | bytes 196616 | tf_op jit(solution)/shard_map/ppermute | solution.py:34
  19.8 8.1 %collective-permute-start.1 = (f32[1,16384]{1,0:T(1,128)S(1)}, f32[1,16384]{1,0:T(1,128)S(1)}, u32[]{:S(2)}, u32[]{:S(2)}) collective-permute-start(f32[1,16384]{1,0:T(1,128)S(1)} %get-tuple-element.47), channel_id=1, source_target_pairs={{0,8},{4,12},{8,0},{12,4},{1,9},{5,13},{9,1},{13,5},{2,10},{6,14},... | collective-permute-start | bytes 196616 | tf_op jit(solution)/shard_map/ppermute | solution.py:34
  20.0 7.9 %collective-permute-start = (f32[1,16384]{1,0:T(1,128)S(1)}, f32[1,16384]{1,0:T(1,128)S(1)}, u32[]{:S(2)}, u32[]{:S(2)}) collective-permute-start(f32[1,16384]{1,0:T(1,128)S(1)} %get-tuple-element.48), channel_id=1, source_target_pairs={{0,4},{4,0},{8,12},{12,8},{1,5},{5,1},{9,13},{13,9},{2,6},{6,2},{1... | collective-permute-start | bytes 196616 | tf_op jit(solution)/shard_map/ppermute | solution.py:34
  24.4 10.2 %all-to-all-start.1 = ((f32[4,1,16384]{2,1,0:T(1,128)}), f32[4,1,16384]{2,1,0:T(1,128)S(1)}, u32[]{:S(2)}, u32[]{:S(2)}) async-start(f32[4,1,16384]{2,1,0:T(1,128)} %copy.4), calls=%async_computation.1 | async-start | bytes 524288 | tf_op jit(solution)/shard_map/all_to_all | solution.py:120
  35.5 1.0 copy-start
  40.1 4.4 %collective-permute-start.3 = (f32[1,2,16,1,1024]{4,3,2,1,0:T(1,128)S(1)}, f32[1,2,16,1,1024]{4,3,2,1,0:T(1,128)S(1)}, u32[]{:S(2)}, u32[]{:S(2)}) collective-permute-start(f32[1,2,16,1,1024]{4,3,2,1,0:T(1,128)S(1)} %get-tuple-element.37), channel_id=1, source_target_pairs={{1,0},{2,1},{3,2},{5,4},{6,5},{7,6},{9,8},{10,9},{11,10},{13,12},{... | collective-permute-start | bytes 393224 | tf_op jit(solution)/shard_map/ppermute | solution.py:47
  41.4 4.0 %collective-permute-start.4 = (f32[1,2,16,1,1024]{4,3,2,1,0:T(1,128)S(1)}, f32[1,2,16,1,1024]{4,3,2,1,0:T(1,128)S(1)}, u32[]{:S(2)}, u32[]{:S(2)}) collective-permute-start(f32[1,2,16,1,1024]{4,3,2,1,0:T(1,128)S(1)} %get-tuple-element.38), channel_id=1, source_target_pairs={{0,1},{1,2},{2,3},{4,5},{5,6},{6,7},{8,9},{9,10},{10,11},{12,13},{... | collective-permute-start | bytes 393224 | tf_op jit(solution)/shard_map/ppermute | solution.py:46
  48.1 6.3 %collective-permute-start.5 = (f32[1,2,16,1,1024]{4,3,2,1,0:T(1,128)S(1)}, f32[1,2,16,1,1024]{4,3,2,1,0:T(1,128)S(1)}, u32[]{:S(2)}, u32[]{:S(2)}) collective-permute-start(f32[1,2,16,1,1024]{4,3,2,1,0:T(1,128)S(1)} %get-tuple-element.31), channel_id=1, source_target_pairs={{1,0},{2,1},{3,2},{5,4},{6,5},{7,6},{9,8},{10,9},{11,10},{13,12},{... | collective-permute-start | bytes 393224 | tf_op jit(solution)/shard_map/ppermute | solution.py:47
  49.4 5.6 %collective-permute-start.6 = (f32[1,2,16,1,1024]{4,3,2,1,0:T(1,128)S(1)}, f32[1,2,16,1,1024]{4,3,2,1,0:T(1,128)S(1)}, u32[]{:S(2)}, u32[]{:S(2)}) collective-permute-start(f32[1,2,16,1,1024]{4,3,2,1,0:T(1,128)S(1)} %get-tuple-element.32), channel_id=1, source_target_pairs={{0,1},{1,2},{2,3},{4,5},{5,6},{6,7},{8,9},{9,10},{10,11},{12,13},{... | collective-permute-start | bytes 393224 | tf_op jit(solution)/shard_map/ppermute | solution.py:46
  57.7 7.4 %collective-permute-start.7 = (f32[1,2,16,1,1024]{4,3,2,1,0:T(1,128)S(1)}, f32[1,2,16,1,1024]{4,3,2,1,0:T(1,128)S(1)}, u32[]{:S(2)}, u32[]{:S(2)}) collective-permute-start(f32[1,2,16,1,1024]{4,3,2,1,0:T(1,128)S(1)} %get-tuple-element.25), channel_id=1, source_target_pairs={{1,0},{2,1},{3,2},{5,4},{6,5},{7,6},{9,8},{10,9},{11,10},{13,12},{... | collective-permute-start | bytes 393224 | tf_op jit(solution)/shard_map/ppermute | solution.py:47
  59.0 6.9 %collective-permute-start.8 = (f32[1,2,16,1,1024]{4,3,2,1,0:T(1,128)S(1)}, f32[1,2,16,1,1024]{4,3,2,1,0:T(1,128)S(1)}, u32[]{:S(2)}, u32[]{:S(2)}) collective-permute-start(f32[1,2,16,1,1024]{4,3,2,1,0:T(1,128)S(1)} %get-tuple-element.26), channel_id=1, source_target_pairs={{0,1},{1,2},{2,3},{4,5},{5,6},{6,7},{8,9},{9,10},{10,11},{12,13},{... | collective-permute-start | bytes 393224 | tf_op jit(solution)/shard_map/ppermute | solution.py:46
  69.1 10.3 %all-to-all-start.2 = ((f32[1,4,16384]{2,0,1:T(1,128)}), f32[1,4,16384]{2,0,1:T(1,128)S(1)}, u32[]{:S(2)}, u32[]{:S(2)}) async-start(f32[1,4,16384]{2,0,1:T(1,128)} %all_to_all.58), calls=%async_computation.2 | async-start | bytes 524288 | tf_op jit(solution)/shard_map/all_to_all | solution.py:138
  79.4 13.9 %all-to-all-start.3 = ((f32[1,4,16384]{2,0,1:T(1,128)}), f32[1,4,16384]{2,0,1:T(1,128)S(1)}, u32[]{:S(2)}, u32[]{:S(2)}) async-start(f32[1,4,16384]{2,0,1:T(1,128)} %all_to_all.61), calls=%async_computation.3 | async-start | bytes 524288 | tf_op jit(solution)/shard_map/all_to_all | solution.py:139
  95.0 14.1 %all-to-all-start.4 = ((f32[4,1,16384]{2,1,0:T(1,128)}), f32[4,1,16384]{2,1,0:T(1,128)S(1)}, u32[]{:S(2)}, u32[]{:S(2)}) async-start(f32[4,1,16384]{2,1,0:T(1,128)} %copy.5), calls=%async_computation.4 | async-start | bytes 524288 | tf_op jit(solution)/shard_map/all_to_all | solution.py:142
